TPU v7x, 32 devices: a whole 2x2x4 slice. The times are simulated.
32 devices in a mesh: groups: 2 (over y), dp: 8 (over z, x), mp: 2 (over core).
Axes of the slice: x: 2, y: 2, z: 4, core: 2. Of those that a mesh axis runs over, the one named last changes fastest.
Arguments:
- tokens: bfloat16 [2048, 4096], P(('groups', 'dp'), 'mp'), parts along dimension 0, may hold values from -6 to 6
- cotangent: bfloat16 [2048, 4096], P(('groups', 'dp'), 'mp'), parts along dimension 0, may hold values from -6 to 6
- gate_spectra: bfloat16 [28, 8, 512], P('mp'), may hold values from -1.5 to 1.5
- up_spectra: bfloat16 [28, 8, 512], P('mp'), may hold values from -1.5 to 1.5
- down_spectra: bfloat16 [8, 28, 512], P('mp'), may hold values from -0.75 to 0.75
Outputs:
- grad_tokens: bfloat16 [2048, 4096], P(('groups', 'dp'), 'mp'), parts along dimension 0
- grad_gate: float32 [56, 8, 512], P(('groups', 'mp')), parts along dimension 0
- grad_up: float32 [56, 8, 512], P(('groups', 'mp')), parts along dimension 0
- grad_down: float32 [16, 28, 512], P(('groups', 'mp')), parts along dimension 0
There are 2 independent parts, one for each index of `groups`. A program takes and returns all parts, laid end to end along the dimension named above; an argument that names none is the same for every part. Nothing has to cross between parts.
All inputs are finite; a program needn't handle non-finite values.
Results may differ from a plain program's by a relative error of at most 0.012.
The roundings to bfloat16 on the way count: a program that leaves them out, or rounds other values in their place, can miss the bound.
Values may be sent and summed in bfloat16 or wider, within the bound.
No kernel may reach another device: no remote copies, remote signals or barrier semaphores. Data moves between devices by JAX's collectives and lax.ppermute only.
A program may use at most 128 MiB of HBM per device.

v0:
```python
import functools
import math

import jax
import jax.numpy as jnp
import numpy as np
from jax import lax
from jax.experimental import pallas as pl
from jax.experimental.pallas import tpu as pltpu
from jax.sharding import PartitionSpec as P


F = 8
PAIR = 2 * F
LANES = 128
ROWS = 16


def transform_tables(block):
    half = block // 2
    n = np.arange(block)
    k = np.arange(half)
    angles = ((n[:, None] * k[None, :]) % block).astype(np.float32) * np.float32(2.0 * math.pi / block)
    cosine = np.cos(angles.astype(np.float64)).astype(np.float32)
    sine = np.sin(angles.astype(np.float64)).astype(np.float32)
    parity = (1 - 2 * (n % 2)).astype(np.float32)
    norm = np.float32(1.0 / math.sqrt(block))
    forward = np.concatenate([cosine, parity[:, None], -sine[:, 1:]], axis=1) * norm
    doubling = np.where(k >= 1, 2.0, 1.0).astype(np.float32)
    inverse = np.concatenate([(cosine * doubling).T, parity[None, :], -2.0 * sine[:, 1:].T], axis=0) * norm
    order = np.arange(block).reshape(2, half // PAIR, PAIR).transpose(1, 0, 2).reshape(-1)
    extra = np.zeros((16, half), np.float32)
    folded = np.concatenate([np.arange(half), [half], np.arange(block - 1, half, -1)])
    forward_cos = np.concatenate([forward[:half, :half].T, extra], axis=0)
    forward_cos[half] = forward[:half, half]
    forward_sin = forward[:half, half:].T.copy()
    forward_sin[0] = 0.0
    natural = inverse.T[:, order]
    tables = (forward.T[order], natural, natural[folded], forward_cos, forward_sin)
    return [jnp.asarray(table, jnp.bfloat16) for table in tables]


def nt_dot(a, b):
    return lax.dot_general(a, b, (((1,), (1,)), ((), ())), preferred_element_type=jnp.float32)


def dot(a, b):
    return jnp.dot(a, b, preferred_element_type=jnp.float32)


def swap_blocks(tiles):
    tiles = list(tiles)
    lane_block = lax.broadcasted_iota(jnp.int32, tiles[0].shape, 1) // F
    step = len(tiles) // 2
    while step:
        high = (lane_block & step) != 0
        for i in range(len(tiles)):
            if i & step:
                continue
            low_tile, high_tile = tiles[i], tiles[i + step]
            tiles[i] = jnp.where(high, pltpu.roll(high_tile, F * step, 1), low_tile)
            tiles[i + step] = jnp.where(high, high_tile, pltpu.roll(low_tile, LANES - F * step, 1))
        step //= 2
    return tiles


def weight_rows(read, write, conj, half):
    for part in range(half // LANES):
        at = part * LANES
        tiles = swap_blocks([read(i, at) for i in range(8)] + [read(i, half + at) for i in range(8)])
        for i, tile in enumerate(tiles):
            lane = lax.broadcasted_iota(jnp.int32, tile.shape, 1)
            left = lane < LANES // 2
            turned = pltpu.roll(tile, LANES // 2, 1)
            if conj:
                real, imag = tile, jnp.where(left, -turned, turned)
            else:
                real, imag = jnp.where(left, tile, -tile), turned
            if part == 0 and i == 0:
                first = lane % F == 0
                real = jnp.where(first & ~left, 0.0, real)
                imag = jnp.where(first, jnp.where(left, 0.0, tile), imag)
            write(part * 16 + i, 0, real)
            write(part * 16 + i, 1, imag)


def adjoint_rows(read, write, half):
    for part in range(half // LANES):
        at = part * LANES
        re = swap_blocks([read(o, at) for o in range(16)])
        im = swap_blocks([read(o, half + at) for o in range(16)])
        for i in range(16):
            cross, wim = re[i], im[i]
            if part == 0 and i == 0:
                first = lax.broadcasted_iota(jnp.int32, wim.shape, 1) % F == 0
                cross = jnp.where(first, wim, cross)
                wim = jnp.where(first, 0.0, wim)
            write(part * 16 + i, 0, 0, re[i])
            write(part * 16 + i, 0, 1, wim)
            write(part * 16 + i, 1, 0, -wim)
            write(part * 16 + i, 1, 1, cross)


def diagonal():
    row = lax.broadcasted_iota(jnp.int32, (PAIR, LANES), 0)
    lane = lax.broadcasted_iota(jnp.int32, (PAIR, LANES), 1)
    return jnp.where(lane % F == row % F, 1.0, 0.0).astype(jnp.bfloat16)


def spread(read, count, mask):
    return jnp.concatenate(
        [jnp.concatenate([read(r), read(r + 1)], axis=0).astype(jnp.bfloat16) * mask for r in range(0, count, 2)], axis=0
    )


def blocks(first, second):
    zero = jnp.zeros_like(first)
    return jnp.concatenate(
        [jnp.concatenate([first, zero], axis=1), jnp.concatenate([zero, second], axis=1)], axis=0
    )


def side_by_side(values):
    return jnp.concatenate([values[..., :LANES], values[..., LANES:]], axis=-2)


def swiglu_back(gate, up, grad):
    sig = 1.0 / (1.0 + jnp.exp(-gate))
    gated = gate * sig
    slope = sig + gated * (1.0 - sig)
    return (
        (gated * up).astype(jnp.bfloat16),
        (grad * up * slope).astype(jnp.bfloat16),
        (grad * gated).astype(jnp.bfloat16),
    )


def main_kernel(fb, norm, wg_in, wu_in, pt_in, x_own_in, c_own_in, wd_own_in, wd_other_in, x_other_in, c_other_in,
                qf_in, pc_in, ps_in, d_out, gg_out, ug_out, wg_ref, wu_ref, pt_ref, x_own, c_own, wd_ref,
                x_other, c_other, qf_ref, pc_ref, ps_ref, sx, sc, gs, us, hs, hid, gg, ug, rg, ru, rd,
                sums_ref, diffs_ref, mids_ref, flat, flat_down, d_ref, in_sem, out_sem, d_sem):
    core = lax.axis_index("mp")
    db = 8
    per = db // 2
    block = pt_ref.shape[0]
    half = block // 2
    pairs = half // PAIR
    arrays = (
        (wg_in, wg_ref), (wu_in, wu_ref), (pt_in, pt_ref), (x_own_in, x_own), (c_own_in, c_own),
        (wd_own_in, wd_ref.at[core]), (wd_other_in, wd_ref.at[1 - core]),
        (x_other_in, x_other), (c_other_in, c_other),
        (qf_in, qf_ref), (pc_in, pc_ref), (ps_in, ps_ref),
    )
    copies = [pltpu.make_async_copy(src, dst, in_sem.at[n]) for n, (src, dst) in enumerate(arrays)]
    for copy in copies:
        copy.start()

    def to_spectra(source, target, first):
        rows = jnp.concatenate([source[:, j * block : (j + 1) * block] for j in range(per)], axis=0)
        result = nt_dot(pt_ref[...], rows).reshape(pairs, 2, 2, F, per * LANES)
        for j in range(0, per, 2):
            two = side_by_side(result[..., j * LANES : (j + 2) * LANES])
            target[:, :, :, first // 2 + j // 2] = two.astype(jnp.bfloat16)

    for copy in copies[:5]:
        copy.wait()
    to_spectra(x_own, sx, core * per)
    to_spectra(c_own, sc, core * per)
    for n, (source, target) in enumerate(((wg_ref, rg), (wu_ref, ru))):
        for tile in range(block // LANES):
            for o in range(fb):
                flat[n, tile, o * db : (o + 1) * db] = source[o, :, tile * LANES : (tile + 1) * LANES].astype(jnp.float32)

        def read(i, at, n=n):
            return flat[n, at // LANES, pl.ds(i, fb, stride=db), :]

        def write(group, ri, rows, target=target):
            at = (group * 2 + ri) * ROWS
            target[at : at + fb, :] = rows

        weight_rows(read, write, False, half)

    for copy in copies[5:9]:
        copy.wait()
    to_spectra(x_other, sx, (1 - core) * per)
    to_spectra(c_other, sc, (1 - core) * per)

    for o in range(db):
        for tile in range(block // LANES):
            flat_down[tile, o] = wd_ref[o // per, :, o % per, tile * LANES : (tile + 1) * LANES].astype(jnp.float32)

    def read_down(o, at):
        return flat_down[at // LANES, o, pl.ds(core * fb, fb), :]

    def write_down(group, ri, rows):
        at = (group * 2 + ri) * ROWS
        rd[at : at + fb, :] = rows

    weight_rows(read_down, write_down, True, half)
    if fb < ROWS:
        for target in (gg, ug):
            target[:, :, :, fb // 2 :] = jnp.zeros((pairs, 2, 2, (ROWS - fb) // 2, PAIR, LANES), jnp.bfloat16)

    mask = diagonal()

    def both_groups(ref, g):
        return blocks(*(ref[g, :, h].reshape(LANES, LANES) for h in range(2)))

    def mix(g):
        for source, weights in ((sx, ((rg, gs), (ru, us))), (sc, ((rd, hs),))):
            spectrum = both_groups(source, g)
            for rows, target in weights:
                wide = jnp.concatenate(
                    [
                        jnp.concatenate(
                            [
                                spread(
                                    lambda o, h=h, ri=ri, rows=rows: rows[
                                        pl.ds(((2 * g + h) * 2 + ri) * ROWS + o, F, stride=0), :
                                    ],
                                    fb,
                                    mask,
                                )
                                for h in range(2)
                            ],
                            axis=1,
                        )
                        for ri in range(2)
                    ],
                    axis=0,
                )
                result = side_by_side(dot(wide, spectrum).reshape(2, fb, F, 2 * LANES)).astype(jnp.bfloat16)
                for ri in range(2):
                    target[:, g, ri] = result[ri]

    @pl.loop(0, pairs // 4)
    def _(n):
        for u in range(4):
            mix(4 * n + u)

    for copy in copies[9:]:
        copy.wait()
    top = lax.broadcasted_iota(jnp.int32, (F, LANES), 0)
    wide_top = lax.broadcasted_iota(jnp.int32, (F, 2 * LANES), 0)
    signed = jnp.where(wide_top % 2 == 0, norm, -norm)
    inner = jnp.where(lax.broadcasted_iota(jnp.int32, (PAIR, 2 * LANES), 0) == 0, 0.0, 1.0).astype(jnp.bfloat16)

    def set_row(values, row):
        return jnp.concatenate([jnp.where(wide_top == 0, row, values[:F]), values[F:]], axis=0)

    def add_tile(values, tile):
        return (values.reshape(-1, F, 2 * LANES) + tile[None]).reshape(values.shape)

    def to_values(pair):
        spectra = jnp.concatenate(
            [ref[2 * pair + u].reshape(block, LANES) for ref in (gs, us, hs) for u in range(2)], axis=1
        )
        return dot(qf_ref[...], spectra)

    def to_grads(values, slot):
        gate, up, grad = (values[:, v * 2 * LANES : (v + 1) * 2 * LANES] for v in range(3))
        for v, side in enumerate(swiglu_back(gate, up, grad)):
            near, far = side[:half], side[half:]
            mids_ref[slot, v] = far[:PAIR].astype(jnp.float32)[:F]
            sums_ref[slot, v, :PAIR] = near[:PAIR] + far[:PAIR] * inner
            sums_ref[slot, v, PAIR:] = near[PAIR:] + far[PAIR:]
            diffs_ref[slot, v] = near - far

    def to_grad_spectra(pair, slot):
        re = dot(pc_ref[...], jnp.concatenate([sums_ref[slot, v] for v in range(3)], axis=1))
        im = dot(ps_ref[...], jnp.concatenate([diffs_ref[slot, v] for v in range(3)], axis=1))
        for v, target in enumerate((hid, gg, ug)):
            lanes = slice(v * 2 * LANES, (v + 1) * 2 * LANES)
            middle = mids_ref[slot, v][:1]
            real = add_tile(re[:half, lanes], middle * signed)
            imag = set_row(im[:, lanes], re[half : half + 1, lanes] + middle * norm)
            for ri, both in enumerate((real, imag)):
                target[:, ri, :, pair] = side_by_side(both.reshape(pairs, 2, F, 2 * LANES)).astype(jnp.bfloat16)

    steps = fb // 2
    to_grads(to_values(0), 0)

    @pl.loop(0, (steps - 1) // 2)
    def _(n):
        for u in range(2):
            values = to_values(2 * n + u + 1)
            to_grad_spectra(2 * n + u, u)
            to_grads(values, 1 - u)

    if steps % 2 == 0:
        to_grad_spectra(steps - 2, 0)
        to_grads(to_values(steps - 1), 1)
    to_grad_spectra(steps - 1, 1 - steps % 2)

    stores = [
        pltpu.make_async_copy(src, dst, out_sem.at[n]) for n, (src, dst) in enumerate(((gg, gg_out), (ug, ug_out)))
    ]
    for copy in stores:
        copy.start()
    lane = lax.broadcasted_iota(jnp.int32, (F, LANES), 1)
    left = lane < LANES // 2

    def weight_sums(g):
        for w, (rows, cols, sign) in enumerate(((gg, sx, 1), (ug, sx, 1), (hid, sc, -1))):
            two = jnp.concatenate([rows[g, :, h, : fb // 2].reshape(2 * fb * F, LANES) for h in range(2)], axis=1)
            m = nt_dot(two, both_groups(cols, g))
            for h in range(2):
                result = []
                for upper in range(0, fb, 8):
                    sums = [jnp.zeros((F, LANES), jnp.float32)] * 2
                    for o in range(upper, min(upper + 8, fb)):
                        turn = o - upper
                        here = (top - lane) % 8 == turn
                        for q in range(2):
                            tile = m[(q * fb + o) * F : (q * fb + o + 1) * F, h * LANES : (h + 1) * LANES]
                            sums[q] = jnp.where(here, pltpu.roll(tile, turn, 0) if turn else tile, sums[q])
                    same = jnp.where(left, sums[0], sums[1])
                    cross = jnp.where(left, sums[1], sums[0])
                    turned = pltpu.roll(cross, LANES // 2, 1)
                    both = jnp.where(
                        left, same + pltpu.roll(same, LANES // 2, 1), turned - cross if sign > 0 else cross - turned
                    )
                    if h == 0:
                        both = jnp.where((lane % F == 0) & (g == 0), same, both)
                    result.append(both)
                d_ref[g, w * ROWS : (w + 1) * ROWS, h * LANES : (h + 1) * LANES] = jnp.concatenate(
                    result, axis=0
                ).astype(jnp.bfloat16)

    def sums_copy(n):
        rows = pl.ds(4 * n, 4)
        return pltpu.make_async_copy(d_ref.at[rows], d_out.at[rows], d_sem.at[n])

    @pl.loop(0, pairs // 4)
    def _(n):
        for u in range(4):
            weight_sums(4 * n + u)
        sums_copy(n).start()

    for n in range(pairs // 4):
        sums_copy(n).wait()
    for copy in stores:
        copy.wait()


def adjoint_kernel(fb, wg_in, wu_in, gg_in, ug_in, own_out, other_out, wg_ref, wu_ref, gg, ug, ra, rb, part, own_ref,
                   other_ref, in_sem, g_sem, out_sem):
    core = lax.axis_index("mp")
    db = 8
    per = db // 2
    pairs = gg.shape[0]
    half = pairs * PAIR
    weights = [
        pltpu.make_async_copy(src, dst, in_sem.at[n]) for n, (src, dst) in enumerate(((wg_in, wg_ref), (wu_in, wu_ref)))
    ]

    def group_copies(g):
        return [
            pltpu.make_async_copy(src.at[g], dst.at[g], g_sem.at[n, g])
            for n, (src, dst) in enumerate(((gg_in, gg), (ug_in, ug)))
        ]

    def results(n):
        rows = pl.ds(2 * n, 2)
        return [
            pltpu.make_async_copy(src.at[rows], dst.at[rows], out_sem.at[k, n])
            for k, (src, dst) in enumerate(((own_ref, own_out), (other_ref, other_out)))
        ]

    for copy in weights:
        copy.start()
    for g in range(pairs):
        for copy in group_copies(g):
            copy.start()
    for copy in weights:
        copy.wait()
    for source, adjoint in ((wg_ref, ra), (wu_ref, rb)):
        def read(o, at, source=source):
            if o >= fb:
                return jnp.zeros((db, LANES), jnp.float32)
            return source[o, :, at : at + LANES].astype(jnp.float32)

        def write(group, ri, tile, rows, adjoint=adjoint):
            at = (group * 2 + ri) * db
            adjoint[tile, at : at + db, :] = rows

        adjoint_rows(read, write, half)
    mask = diagonal()

    def mix(g, slot):
        spectrum = jnp.concatenate([blocks(*(ref[g, :, h].reshape(2 * LANES, LANES) for h in range(2))) for ref in (gg, ug)])
        wide = jnp.concatenate(
            [
                spread(
                    lambda r, h=h, tile=tile, ref=ref: ref[tile, pl.ds((2 * g + h) * 2 * db + r, F, stride=0), :],
                    2 * db,
                    mask,
                )
                for ref in (ra, rb)
                for h in range(2)
                for tile in range(2)
            ],
            axis=1,
        )
        part[slot] = side_by_side(dot(wide, spectrum).reshape(2, db, F, 2 * LANES))
        for ri in range(2):
            own_ref[g, ri] = part[slot, ri, pl.ds(core * per, per)]
            other_ref[g, ri] = part[slot, ri, pl.ds((1 - core) * per, per)].astype(jnp.bfloat16)

    @pl.loop(0, pairs // 2)
    def _(n):
        for u in range(2):
            for copy in group_copies(2 * n + u):
                copy.wait()
        for u in range(2):
            mix(2 * n + u, u)
        for copy in results(n):
            copy.start()

    for n in range(pairs // 2):
        for copy in results(n):
            copy.wait()


def input_kernel(qt_in, own_in, got_in, out_ref, qt_ref, own_ref, got_ref, in_sem):
    block = qt_ref.shape[0]
    copies = [
        pltpu.make_async_copy(src, dst, in_sem.at[n])
        for n, (src, dst) in enumerate(((qt_in, qt_ref), (own_in, own_ref), (got_in, got_ref)))
    ]
    for copy in copies:
        copy.start()
    for copy in copies:
        copy.wait()
    spectra = (own_ref[...] + got_ref[...].astype(jnp.float32)).astype(jnp.bfloat16)
    for j in range(0, own_ref.shape[2], 2):
        two = jnp.concatenate([spectra[:, :, j + u].reshape(block, LANES) for u in range(2)], axis=1)
        values = dot(qt_ref[...], two)
        for u in range(2):
            out_ref[:, (j + u) * block : (j + u + 1) * block] = values[:, u * LANES : (u + 1) * LANES].T.astype(jnp.bfloat16)


def straight(tile):
    halves = []
    lane = lax.broadcasted_iota(jnp.int32, (8, LANES), 1)
    for at in range(0, tile.shape[0], 8):
        half = tile[at : at + 8]
        for bit in (1, 2, 4):
            half = jnp.where((lane & bit) != 0, pltpu.roll(half, 8 - bit, 0), half)
        halves.append(half)
    return jnp.concatenate(halves, axis=0)


def reduce_kernel(r_ref, out_ref):
    for g in range(r_ref.shape[1]):
        for lanes in (slice(0, LANES), slice(LANES, 2 * LANES)):
            total = r_ref[0, g, :, lanes].astype(jnp.float32)
            for d in range(1, r_ref.shape[0]):
                total = total + r_ref[d, g, :, lanes].astype(jnp.float32)
            total = straight(total).astype(jnp.bfloat16)
            for d in range(out_ref.shape[0]):
                out_ref[d, g, :, lanes] = total


def entries(source, rows, part):
    tiles = []
    for i in range(16):
        lanes = slice((i % 2) * LANES, (i % 2 + 1) * LANES)
        tiles.append(source[part * 8 + i // 2, rows, lanes].astype(jnp.float32))
    return swap_blocks(tiles)


def factor(scale, part):
    lane = lax.broadcasted_iota(jnp.int32, (1, LANES), 1)
    return jnp.where((lane == 0) & (part == 0), scale, 2.0 * scale)


def layout_kernel(scale, fb, s_ref, gate_ref, up_ref, flat):
    half = s_ref.shape[0] * PAIR
    for w, target in enumerate((gate_ref, up_ref)):
        for part in range(half // LANES):
            tiles = entries(s_ref, slice(w * ROWS, (w + 1) * ROWS), part)
            for ri in range(2):
                at = ri * half + part * LANES
                for i in range(8):
                    flat[w, ri, pl.ds(i, fb, stride=8), :] = tiles[8 * ri + i][:fb] * factor(scale, part)
                target[:, at : at + LANES] = flat[w, ri]


def down_layout_kernel(scale, fb, own_ref, got_ref, down_ref):
    core = lax.axis_index("mp")
    half = own_ref.shape[0] * PAIR
    outputs = down_ref.shape[1]
    for source, h in ((own_ref, core), (got_ref, 1 - core)):
        for part in range(half // LANES):
            tiles = entries(source, slice(0, ROWS), part)
            for ri in range(2):
                at = ri * half + part * LANES
                for o in range(outputs):
                    rows = jnp.where(core == 0, tiles[8 * ri + o], tiles[8 * ri + outputs + o])
                    down_ref[pl.ds(h * fb, fb), o, at : at + LANES] = rows[:fb] * factor(scale, part)


ALL_VMEM = 67043328


VMEM = pl.BlockSpec(memory_space=pltpu.VMEM)
HBM = pl.BlockSpec(memory_space=pltpu.HBM)


def call(kernel, out_shape, args, scratch=(), limit=16 << 20, flops=0, moved=0, in_specs=None, out_specs=None):
    return pl.pallas_call(
        kernel,
        out_shape=out_shape,
        in_specs=in_specs or [VMEM] * len(args),
        out_specs=out_specs or jax.tree.map(lambda _: VMEM, out_shape),
        scratch_shapes=list(scratch),
        compiler_params=pltpu.CompilerParams(vmem_limit_bytes=limit),
        cost_estimate=pl.CostEstimate(flops=flops, bytes_accessed=moved, transcendentals=0),
    )(*args)


def shards(tokens, cotangent, gate_spectra, up_spectra, down_spectra):
    n_dp = lax.axis_size("dp")
    swap = [(0, 1), (1, 0)]
    fb, db, block = gate_spectra.shape
    assert db == 8 and fb <= ROWS and fb % 2 == 0 and tokens.shape[0] == LANES and lax.axis_size("mp") == 2
    half = block // 2
    pairs = half // PAIR
    groups = half // F
    per = db // 2
    bf16, f32 = jnp.bfloat16, jnp.float32
    shape = jax.ShapeDtypeStruct
    pt, qt, qf, pc, ps = transform_tables(block)
    norm = float(np.asarray(1.0 / math.sqrt(block), jnp.bfloat16))

    tokens_other = lax.ppermute(tokens, "mp", swap)
    cotangent_other = lax.ppermute(cotangent, "mp", swap)
    down_own = down_spectra.transpose(1, 0, 2)
    down_got = lax.ppermute(down_own, "mp", swap)

    inputs = (
        gate_spectra, up_spectra, pt, tokens, cotangent, down_own, down_got, tokens_other, cotangent_other, qf, pc, ps
    )
    buffers = [shape((2,) + down_own.shape, bf16) if n == 5 else a for n, a in enumerate(inputs) if n != 6]
    spec = shape((pairs, 2, 2, ROWS // 2, PAIR, LANES), bf16)
    d_all, gg, ug = call(
        functools.partial(main_kernel, fb, norm),
        (shape((pairs, 3 * ROWS, 2 * LANES), bf16), spec, spec),
        inputs,
        [pltpu.VMEM(a.shape, bf16) for a in buffers]
        + [pltpu.VMEM((pairs, 2, 2, db // 2, PAIR, LANES), bf16)] * 2
        + [pltpu.VMEM((fb, pairs, 2, PAIR, LANES), bf16)] * 3
        + [pltpu.VMEM(spec.shape, bf16)] * 3
        + [pltpu.VMEM((groups * 2 * ROWS, LANES), f32)] * 3
        + [pltpu.VMEM((2, 3, half, 2 * LANES), bf16)] * 2
        + [pltpu.VMEM((2, 3, F, 2 * LANES), f32), pltpu.VMEM((2, block // LANES, fb * db, LANES), f32)]
        + [pltpu.VMEM((block // LANES, db, 2 * fb, LANES), f32), pltpu.VMEM((pairs, 3 * ROWS, 2 * LANES), bf16)]
        + [pltpu.SemaphoreType.DMA((n,)) for n in (len(inputs), 2, pairs // 4)],
        limit=ALL_VMEM,
        flops=10**10,
        moved=10**7,
        in_specs=[HBM] * len(inputs),
        out_specs=(HBM, HBM, HBM),
    )

    direct = pairs % n_dp == 0
    if direct:
        share = pairs // n_dp
        got = lax.all_to_all(d_all.reshape(n_dp, share, 3 * ROWS, 2 * LANES), "dp", 0, 0, tiled=True)
    else:
        share = pairs
        got = lax.psum(d_all.astype(f32), "dp")[None]
    own, other = call(
        functools.partial(adjoint_kernel, fb),
        (shape((pairs, 2, per, PAIR, LANES), f32), shape((pairs, 2, per, PAIR, LANES), bf16)),
        (gate_spectra, up_spectra, gg, ug),
        [pltpu.VMEM(gate_spectra.shape, bf16)] * 2
        + [pltpu.VMEM(spec.shape, bf16)] * 2
        + [pltpu.VMEM((2, groups * 2 * db, LANES), f32)] * 2
        + [pltpu.VMEM((2, 2, db, PAIR, LANES), f32)]
        + [pltpu.VMEM((pairs, 2, per, PAIR, LANES), t) for t in (f32, bf16)]
        + [pltpu.SemaphoreType.DMA(n) for n in ((2,), (2, pairs), (2, pairs // 2))],
        limit=63 << 20,
        flops=2 * 10**9,
        moved=10**7,
        in_specs=[HBM] * 4,
        out_specs=(HBM, HBM),
    )
    total = call(reduce_kernel, shape((n_dp if direct else 1, share, 3 * ROWS, 2 * LANES), bf16), (got,), moved=10**6)
    total, own, other = lax.optimization_barrier((total, own, other))
    if direct:
        total = lax.all_to_all(total, "dp", 0, 0, tiled=True)
    partner = lax.ppermute(other, "mp", swap)
    grad_tokens = call(
        input_kernel,
        shape(tokens.shape, bf16),
        (qt, own, partner),
        [pltpu.VMEM(a.shape, a.dtype) for a in (qt, own, partner)] + [pltpu.SemaphoreType.DMA((3,))],
        limit=12 << 20,
        flops=5 * 10**8,
        moved=4 * 10**6,
        in_specs=[HBM] * 3,
    )
    total = total.reshape(pairs, 3 * ROWS, 2 * LANES)
    down_sums = total[:, 2 * ROWS :]
    partner_sums = lax.ppermute(down_sums, "mp", swap)
    scale = 1.0 / math.sqrt(tokens.shape[0] * n_dp)
    gate_grad, up_grad = call(
        functools.partial(layout_kernel, scale, fb),
        (shape((fb * db, block), f32),) * 2,
        (total,),
        [pltpu.VMEM((2, 2, fb * db, LANES), f32)],
        moved=10**6,
    )
    down_grad = call(
        functools.partial(down_layout_kernel, scale, fb),
        shape((2 * fb, per, block), f32),
        (down_sums, partner_sums),
        moved=10**6,
    ).transpose(1, 0, 2)
    return (grad_tokens, gate_grad.reshape(fb, db, block), up_grad.reshape(fb, db, block), down_grad)


def solution(mesh):
    in_specs = (
        P(("groups", "dp"), "mp"),
        P(("groups", "dp"), "mp"),
        P("mp", None, None),
        P("mp", None, None),
        P("mp", None, None),
    )
    out_specs = (
        P(("groups", "dp"), "mp"),
        P(("groups", "mp"), None, None),
        P(("groups", "mp"), None, None),
        P(("groups", "mp"), None, None),
    )
    return jax.shard_map(shards, mesh=mesh, in_specs=in_specs, out_specs=out_specs, check_vma=False)
```

profile of v0, /device:TPU:0, one launch (start us, length us, event | category | flops | bytes accessed | tf_op | source)
XLA Modules:
  0.0 59.4 jit_solution(13477558415264200136)
XLA Ops:
  0.6 0.6 collective-permute-start.1
  1.2 0.1 collective-permute-start.2
  1.3 0.4 collective-permute-start
  1.7 2.3 %collective-permute-done.wd_other_in = bf16[28,4,512]{2,1,0:T(4,128)(2,1)} collective-permute-done((bf16[28,4,512]{2,1,0:T(4,128)(2,1)}, bf16[28,4,512]{2,1,0:T(4,128)(2,1)}, u32[]{:S(2)}, u32[]{:S(2)}) %collective-permute-start) | collective-permute-done | bytes 114720 | tf_op jit(solution)/shard_map/ppermute | solution.py:540
  4.0 0.0 collective-permute-done.1.x_other_in
  4.0 0.0 collective-permute-done.2.c_other_in
  4.0 15.4 %shard_map.129 = (bf16[16,48,256]{2,1,0:T(8,128)(2,1)}, bf16[16,2,2,8,16,128]{5,4,3,2,1,0:T(8,128)(2,1)}, bf16[16,2,2,8,16,128]{5,4,3,2,1,0:T(8,128)(2,1)}) custom-call(bf16[14,8,512]{2,1,0:T(8,128)(2,1)} %wg_in.3, bf16[14,8,512]{2,1,0:T(8,128)(2,1)} %wu_in.3, bf16[512,512]{1,0:T(8,128)(2,1)} %constant.10.clone.pt_in, bf16[128,2048]{1,0:T(8,128)(2,1)} %x_own_in.1, ...), custom_call_target="tpu_custom_call" | custom-call | flops 10000000000 | bytes 10000000 | tf_op jit(solution)/shard_map/pallas_call | solution.py:512
  19.4 7.2 %all-to-all-start = ((bf16[8,2,48,256]{3,2,1,0:T(8,128)(2,1)}), bf16[8,2,48,256]{3,2,1,0:T(8,128)(2,1)S(1)}, u32[]{:S(2)}, u32[]{:S(2)}) async-start(bf16[8,2,48,256]{3,2,1,0:T(8,128)(2,1)} %bitcast.8), calls=%async_computation | async-start | bytes 786432 | tf_op jit(solution)/shard_map/all_to_all | solution.py:570
  26.5 6.7 %shard_map.131 = (f32[16,2,4,16,128]{4,3,2,1,0:T(8,128)}, bf16[16,2,4,16,128]{4,3,2,1,0:T(8,128)(2,1)}) custom-call(bf16[14,8,512]{2,1,0:T(8,128)(2,1)} %wg_in.3, bf16[14,8,512]{2,1,0:T(8,128)(2,1)} %wu_in.3, bf16[16,2,2,8,16,128]{5,4,3,2,1,0:T(8,128)(2,1)} %get-tuple-element.15.gg_in, bf16[16,2,2,8,16,128]{5,4,3,2,1,0:T(8,128)(2,1)} %get-tuple-element.16.ug_in), custom_call_target="tpu_custom_call" | custom-call | flops 2000000000 | bytes 10000000 | tf_op jit(solution)/shard_map/pallas_call | solution.py:512
  33.2 0.0 copy-start
  33.2 0.0 copy-start.1
  33.3 5.3 %all-to-all-done.r_ref = bf16[8,2,48,256]{3,2,1,0:T(8,128)(2,1)S(1)} async-done(((bf16[8,2,48,256]{3,2,1,0:T(8,128)(2,1)}), bf16[8,2,48,256]{3,2,1,0:T(8,128)(2,1)S(1)}, u32[]{:S(2)}, u32[]{:S(2)}) %all-to-all-start) | async-done | bytes 393248 | tf_op jit(solution)/shard_map/all_to_all | solution.py:570
  38.5 0.8 %shard_map.130 = bf16[8,2,48,256]{3,2,1,0:T(8,128)(2,1)} custom-call(bf16[8,2,48,256]{3,2,1,0:T(8,128)(2,1)S(1)} %all-to-all-done.r_ref), custom_call_target="tpu_custom_call" | custom-call | bytes 1000000 | tf_op jit(solution)/shard_map/pallas_call | solution.py:512
  39.4 3.6 %all-to-all-start.1 = ((bf16[8,2,48,256]{3,2,1,0:T(8,128)(2,1)}), bf16[8,2,48,256]{3,2,1,0:T(8,128)(2,1)S(1)}, u32[]{:S(2)}, u32[]{:S(2)}) async-start(bf16[8,2,48,256]{3,2,1,0:T(8,128)(2,1)} %shard_map.130), calls=%async_computation.1 | async-start | bytes 786432 | tf_op jit(solution)/shard_map/all_to_all | solution.py:593
  43.0 0.0 collective-permute-start.3
  43.0 11.9 %all-to-all-done.1 = bf16[8,2,48,256]{3,2,1,0:T(8,128)(2,1)S(1)} async-done(((bf16[8,2,48,256]{3,2,1,0:T(8,128)(2,1)}), bf16[8,2,48,256]{3,2,1,0:T(8,128)(2,1)S(1)}, u32[]{:S(2)}, u32[]{:S(2)}) %all-to-all-start.1) | async-done | bytes 393248 | tf_op jit(solution)/shard_map/all_to_all | solution.py:593
  54.9 0.1 collective-permute-start.4
  54.9 0.0 collective-permute-done.3.got_in
  55.0 0.0 copy-done
  55.0 0.0 copy-done.1
  55.0 1.6 %shard_map.132 = bf16[128,2048]{1,0:T(8,128)(2,1)} custom-call(bf16[512,512]{1,0:T(8,128)(2,1)S(1)} %copy-done.1, f32[16,2,4,16,128]{4,3,2,1,0:T(8,128)S(1)} %copy-done, bf16[16,2,4,16,128]{4,3,2,1,0:T(8,128)(2,1)S(1)} %collective-permute-done.3.got_in), custom_call_target="tpu_custom_call" | custom-call | flops 500000000 | bytes 4000000 | tf_op jit(solution)/shard_map/pallas_call | solution.py:512
  56.6 1.4 %shard_map.133 = (f32[112,512]{1,0:T(8,128)}, f32[112,512]{1,0:T(8,128)}) custom-call(bf16[16,48,256]{2,1,0:T(8,128)(2,1)S(1)} %bitcast.7), custom_call_target="tpu_custom_call" | custom-call | bytes 1000000 | tf_op jit(solution)/shard_map/pallas_call | solution.py:512
  58.0 0.0 collective-permute-done.4.got_ref
  58.0 1.4 %shard_map.134 = f32[28,4,512]{2,1,0:T(4,128)} custom-call(bf16[16,16,256]{2,1,0:T(8,128)(2,1)S(1)} %slice.4.own_ref, bf16[16,16,256]{2,1,0:T(8,128)(2,1)S(1)} %collective-permute-done.4.got_ref), custom_call_target="tpu_custom_call" | custom-call | bytes 1000000 | tf_op jit(solution)/shard_map/pallas_call | solution.py:512
  (1 shorter events, 0.0 us)
Async XLA Ops:
  0.6 3.4 %collective-permute-start.1 = (bf16[128,2048]{1,0:T(8,128)(2,1)}, bf16[128,2048]{1,0:T(8,128)(2,1)}, u32[]{:S(2)}, u32[]{:S(2)}) collective-permute-start(bf16[128,2048]{1,0:T(8,128)(2,1)} %x_own_in.1), channel_id=1, source_target_pairs={{0,1},{1,0},{2,3},{3,2},{4,5},{5,4},{6,7},{7,6},{8,9},{9,8},{10,11... | collective-permute-start | bytes 1572872 | tf_op jit(solution)/shard_map/ppermute | solution.py:537
  1.2 2.8 %collective-permute-start.2 = (bf16[128,2048]{1,0:T(8,128)(2,1)}, bf16[128,2048]{1,0:T(8,128)(2,1)}, u32[]{:S(2)}, u32[]{:S(2)}) collective-permute-start(bf16[128,2048]{1,0:T(8,128)(2,1)} %c_own_in.1), channel_id=1, source_target_pairs={{0,1},{1,0},{2,3},{3,2},{4,5},{5,4},{6,7},{7,6},{8,9},{9,8},{10,11... | collective-permute-start | bytes 1572872 | tf_op jit(solution)/shard_map/ppermute | solution.py:538
  1.3 2.7 %collective-permute-start = (bf16[28,4,512]{2,1,0:T(4,128)(2,1)}, bf16[28,4,512]{2,1,0:T(4,128)(2,1)}, u32[]{:S(2)}, u32[]{:S(2)}) collective-permute-start(bf16[28,4,512]{2,1,0:T(4,128)(2,1)} %bitcast.12), channel_id=1, source_target_pairs={{0,1},{1,0},{2,3},{3,2},{4,5},{5,4},{6,7},{7,6},{8,9},{9,8},{10,11... | collective-permute-start | bytes 344072 | tf_op jit(solution)/shard_map/ppermute | solution.py:540
  19.4 19.2 %all-to-all-start = ((bf16[8,2,48,256]{3,2,1,0:T(8,128)(2,1)}), bf16[8,2,48,256]{3,2,1,0:T(8,128)(2,1)S(1)}, u32[]{:S(2)}, u32[]{:S(2)}) async-start(bf16[8,2,48,256]{3,2,1,0:T(8,128)(2,1)} %bitcast.8), calls=%async_computation | async-start | bytes 786432 | tf_op jit(solution)/shard_map/all_to_all | solution.py:570
  33.2 21.7 %copy-start = (f32[16,2,4,16,128]{4,3,2,1,0:T(8,128)S(1)}, f32[16,2,4,16,128]{4,3,2,1,0:T(8,128)}, u32[]{:S(2)}) copy-start(f32[16,2,4,16,128]{4,3,2,1,0:T(8,128)} %get-tuple-element.19.own_in) | copy-start | bytes 3145732
  33.2 21.7 %copy-start.1 = (bf16[512,512]{1,0:T(8,128)(2,1)S(1)}, bf16[512,512]{1,0:T(8,128)(2,1)}, u32[]{:S(2)}) copy-start(bf16[512,512]{1,0:T(8,128)(2,1)} %constant.11.clone.qt_in) | copy-start | bytes 1572868
  39.4 15.5 %all-to-all-start.1 = ((bf16[8,2,48,256]{3,2,1,0:T(8,128)(2,1)}), bf16[8,2,48,256]{3,2,1,0:T(8,128)(2,1)S(1)}, u32[]{:S(2)}, u32[]{:S(2)}) async-start(bf16[8,2,48,256]{3,2,1,0:T(8,128)(2,1)} %shard_map.130), calls=%async_computation.1 | async-start | bytes 786432 | tf_op jit(solution)/shard_map/all_to_all | solution.py:593
  43.0 12.0 %collective-permute-start.3 = (bf16[16,2,4,16,128]{4,3,2,1,0:T(8,128)(2,1)}, bf16[16,2,4,16,128]{4,3,2,1,0:T(8,128)(2,1)S(1)}, u32[]{:S(2)}, u32[]{:S(2)}) collective-permute-start(bf16[16,2,4,16,128]{4,3,2,1,0:T(8,128)(2,1)} %get-tuple-element.20), channel_id=1, source_target_pairs={{0,1},{1,0},{2,3},{3,2},{4,5},{5,4},{6,7},{7,6},{8,9},{9,8},{10,11... | collective-permute-start | bytes 1572872 | tf_op jit(solution)/shard_map/ppermute | solution.py:594
  54.9 3.1 %collective-permute-start.4 = (bf16[16,16,256]{2,1,0:T(8,128)(2,1)S(1)}, bf16[16,16,256]{2,1,0:T(8,128)(2,1)S(1)}, u32[]{:S(2)}, u32[]{:S(2)}) collective-permute-start(bf16[16,16,256]{2,1,0:T(8,128)(2,1)S(1)} %slice.4.own_ref), channel_id=1, source_target_pairs={{0,1},{1,0},{2,3},{3,2},{4,5},{5,4},{6,7},{7,6},{8,9},{9,8},{10,11... | collective-permute-start | bytes 393224 | tf_op jit(solution)/shard_map/ppermute | solution.py:607
where the time goes:
time: 59.7 us; the launch traced here: 59.4 us
  Pallas kernels  27.3 us (46%)
  waiting for transfers between devices  19.4 us (32%)
  starting transfers between devices  12 us (20%)
  between operations  0.72 us (1%)
    pallas_call x6, Pallas kernels, call(): pl.pallas_call(kernel, out_shape=out_shape, in_specs=in_specs or [VMEM] *...  27.3 us
    all_to_all x1, waiting for transfers between devices, shards(): total = lax.all_to_all(total, 'dp', 0, 0, tiled=True)  11.9 us
    all_to_all x1, starting transfers between devices, shards(): lax.all_to_all(d_all.reshape(n_dp, share, 3 * ROWS, 2 * LANES), 'dp', 0,...  7.17 us
    all_to_all x1, waiting for transfers between devices, shards(): lax.all_to_all(d_all.reshape(n_dp, share, 3 * ROWS, 2 * LANES), 'dp', 0,...  5.27 us
    all_to_all x1, starting transfers between devices, shards(): total = lax.all_to_all(total, 'dp', 0, 0, tiled=True)  3.64 us
    ppermute x1, waiting for transfers between devices, shards(): down_got = lax.ppermute(down_own, 'mp', swap)  2.28 us
  transfers between devices with their start and end apart: 7, of which 3 were waited for; matrix products, arithmetic and copies ran while one was open for 0% of the time, Pallas kernels for 16%

commit v1 on v0

--- a/solution.py
+++ b/solution.py
@@ -185,12 +185,13 @@
     to_spectra(x_other, sx, (1 - core) * per)
     to_spectra(c_other, sc, (1 - core) * per)
 
-    for o in range(db):
+    for side in range(2):
         for tile in range(block // LANES):
-            flat_down[tile, o] = wd_ref[o // per, :, o % per, tile * LANES : (tile + 1) * LANES].astype(jnp.float32)
+            rows = wd_ref[side, :, :, tile * LANES : (tile + 1) * LANES].astype(jnp.float32)
+            flat_down[side, tile] = rows.reshape(2 * fb * per, LANES)
 
     def read_down(o, at):
-        return flat_down[at // LANES, o, pl.ds(core * fb, fb), :]
+        return flat_down[o // per, at // LANES, pl.ds(core * fb * per + o % per, fb, stride=per), :]
 
     def write_down(group, ri, rows):
         at = (group * 2 + ri) * ROWS
@@ -233,10 +234,10 @@
                 for ri in range(2):
                     target[:, g, ri] = result[ri]
 
-    @pl.loop(0, pairs // 4)
+    @pl.loop(0, pairs // 8)
     def _(n):
-        for u in range(4):
-            mix(4 * n + u)
+        for u in range(8):
+            mix(8 * n + u)
 
     for copy in copies[9:]:
         copy.wait()
@@ -328,16 +329,16 @@
                 ).astype(jnp.bfloat16)
 
     def sums_copy(n):
-        rows = pl.ds(4 * n, 4)
+        rows = pl.ds(8 * n, 8)
         return pltpu.make_async_copy(d_ref.at[rows], d_out.at[rows], d_sem.at[n])
 
-    @pl.loop(0, pairs // 4)
+    @pl.loop(0, pairs // 8)
     def _(n):
-        for u in range(4):
-            weight_sums(4 * n + u)
+        for u in range(8):
+            weight_sums(8 * n + u)
         sums_copy(n).start()
 
-    for n in range(pairs // 4):
+    for n in range(pairs // 8):
         sums_copy(n).wait()
     for copy in stores:
         copy.wait()
@@ -493,7 +494,7 @@
     outputs = down_ref.shape[1]
     for source, h in ((own_ref, core), (got_ref, 1 - core)):
         for part in range(half // LANES):
-            tiles = entries(source, slice(0, ROWS), part)
+            tiles = entries(source, slice(2 * ROWS, 3 * ROWS), part)
             for ri in range(2):
                 at = ri * half + part * LANES
                 for o in range(outputs):
@@ -555,8 +556,8 @@
         + [pltpu.VMEM((groups * 2 * ROWS, LANES), f32)] * 3
         + [pltpu.VMEM((2, 3, half, 2 * LANES), bf16)] * 2
         + [pltpu.VMEM((2, 3, F, 2 * LANES), f32), pltpu.VMEM((2, block // LANES, fb * db, LANES), f32)]
-        + [pltpu.VMEM((block // LANES, db, 2 * fb, LANES), f32), pltpu.VMEM((pairs, 3 * ROWS, 2 * LANES), bf16)]
-        + [pltpu.SemaphoreType.DMA((n,)) for n in (len(inputs), 2, pairs // 4)],
+        + [pltpu.VMEM((2, block // LANES, 2 * fb * per, LANES), f32), pltpu.VMEM((pairs, 3 * ROWS, 2 * LANES), bf16)]
+        + [pltpu.SemaphoreType.DMA((n,)) for n in (len(inputs), 2, pairs // 8)],
         limit=ALL_VMEM,
         flops=10**10,
         moved=10**7,
@@ -603,8 +604,7 @@
         in_specs=[HBM] * 3,
     )
     total = total.reshape(pairs, 3 * ROWS, 2 * LANES)
-    down_sums = total[:, 2 * ROWS :]
-    partner_sums = lax.ppermute(down_sums, "mp", swap)
+    partner_sums = lax.ppermute(total, "mp", swap)
     scale = 1.0 / math.sqrt(tokens.shape[0] * n_dp)
     gate_grad, up_grad = call(
         functools.partial(layout_kernel, scale, fb),
@@ -616,7 +616,7 @@
     down_grad = call(
         functools.partial(down_layout_kernel, scale, fb),
         shape((2 * fb, per, block), f32),
-        (down_sums, partner_sums),
+        (total, partner_sums),
         moved=10**6,
     ).transpose(1, 0, 2)
     return (grad_tokens, gate_grad.reshape(fb, db, block), up_grad.reshape(fb, db, block), down_grad)

time: 59.7 us -> 58.6 us (0.982)
  Pallas kernels: 27.3 us -> 26.3 us
    pallas_call x6, Pallas kernels: 27.3 us -> 26.3 us  [call(): pl.pallas_call(kernel, out_shape=out_shape, in_specs=in_specs or [VMEM] *...]
  transfers between devices with their start and end apart: 7 -> 7, of which waited for: 3 -> 3; matrix products, arithmetic and copies ran while one was open for 0% -> 0% of each run, Pallas kernels for 16% -> 17%
where the time goes in v1:
time: 58.6 us; the launch traced here: 58.2 us
  Pallas kernels  26.3 us (45%)
  waiting for transfers between devices  19.4 us (33%)
  starting transfers between devices  11.9 us (20%)
  between operations  0.69 us (1%)
    pallas_call x6, Pallas kernels, call(): pl.pallas_call(kernel, out_shape=out_shape, in_specs=in_specs or [VMEM] *...  26.3 us
    all_to_all x1, waiting for transfers between devices, shards(): total = lax.all_to_all(total, 'dp', 0, 0, tiled=True)  11.9 us
    all_to_all x1, starting transfers between devices, shards(): lax.all_to_all(d_all.reshape(n_dp, share, 3 * ROWS, 2 * LANES), 'dp', 0,...  7.17 us
    all_to_all x1, waiting for transfers between devices, shards(): lax.all_to_all(d_all.reshape(n_dp, share, 3 * ROWS, 2 * LANES), 'dp', 0,...  5.22 us
    all_to_all x1, starting transfers between devices, shards(): total = lax.all_to_all(total, 'dp', 0, 0, tiled=True)  3.64 us
    ppermute x1, waiting for transfers between devices, shards(): down_got = lax.ppermute(down_own, 'mp', swap)  2.28 us
  transfers between devices with their start and end apart: 7, of which 3 were waited for; matrix products, arithmetic and copies ran while one was open for 0% of the time, Pallas kernels for 17%

profile of v1, /device:TPU:0, one launch (start us, length us, event | category | flops | bytes accessed | tf_op | source)
XLA Modules:
  0.0 58.2 jit_solution(15628867715376700677)
XLA Ops:
  0.6 0.6 collective-permute-start.1
  1.2 0.1 collective-permute-start.2
  1.3 0.4 collective-permute-start
  1.7 2.3 %collective-permute-done.wd_other_in = bf16[28,4,512]{2,1,0:T(4,128)(2,1)} collective-permute-done((bf16[28,4,512]{2,1,0:T(4,128)(2,1)}, bf16[28,4,512]{2,1,0:T(4,128)(2,1)}, u32[]{:S(2)}, u32[]{:S(2)}) %collective-permute-start) | collective-permute-done | bytes 114720 | tf_op jit(solution)/shard_map/ppermute | solution.py:541
  4.0 0.0 collective-permute-done.1.x_other_in
  4.0 0.0 collective-permute-done.2.c_other_in
  4.0 14.4 %shard_map.129 = (bf16[16,48,256]{2,1,0:T(8,128)(2,1)}, bf16[16,2,2,8,16,128]{5,4,3,2,1,0:T(8,128)(2,1)}, bf16[16,2,2,8,16,128]{5,4,3,2,1,0:T(8,128)(2,1)}) custom-call(bf16[14,8,512]{2,1,0:T(8,128)(2,1)} %wg_in.3, bf16[14,8,512]{2,1,0:T(8,128)(2,1)} %wu_in.3, bf16[512,512]{1,0:T(8,128)(2,1)} %constant.10.clone.pt_in, bf16[128,2048]{1,0:T(8,128)(2,1)} %x_own_in.1, ...), custom_call_target="tpu_custom_call" | custom-call | flops 10000000000 | bytes 10000000 | tf_op jit(solution)/shard_map/pallas_call | solution.py:513
  18.4 7.2 %all-to-all-start = ((bf16[8,2,48,256]{3,2,1,0:T(8,128)(2,1)}), bf16[8,2,48,256]{3,2,1,0:T(8,128)(2,1)S(1)}, u32[]{:S(2)}, u32[]{:S(2)}) async-start(bf16[8,2,48,256]{3,2,1,0:T(8,128)(2,1)} %bitcast.9), calls=%async_computation | async-start | bytes 786432 | tf_op jit(solution)/shard_map/all_to_all | solution.py:571
  25.5 0.0 copy-start.1
  25.5 6.7 %shard_map.131 = (f32[16,2,4,16,128]{4,3,2,1,0:T(8,128)}, bf16[16,2,4,16,128]{4,3,2,1,0:T(8,128)(2,1)}) custom-call(bf16[14,8,512]{2,1,0:T(8,128)(2,1)} %wg_in.3, bf16[14,8,512]{2,1,0:T(8,128)(2,1)} %wu_in.3, bf16[16,2,2,8,16,128]{5,4,3,2,1,0:T(8,128)(2,1)} %get-tuple-element.15.gg_in, bf16[16,2,2,8,16,128]{5,4,3,2,1,0:T(8,128)(2,1)} %get-tuple-element.16.ug_in), custom_call_target="tpu_custom_call" | custom-call | flops 2000000000 | bytes 10000000 | tf_op jit(solution)/shard_map/pallas_call | solution.py:513
  32.3 0.0 copy-start
  32.3 5.2 %all-to-all-done.r_ref = bf16[8,2,48,256]{3,2,1,0:T(8,128)(2,1)S(1)} async-done(((bf16[8,2,48,256]{3,2,1,0:T(8,128)(2,1)}), bf16[8,2,48,256]{3,2,1,0:T(8,128)(2,1)S(1)}, u32[]{:S(2)}, u32[]{:S(2)}) %all-to-all-start) | async-done | bytes 393248 | tf_op jit(solution)/shard_map/all_to_all | solution.py:571
  37.5 0.8 %shard_map.130 = bf16[8,2,48,256]{3,2,1,0:T(8,128)(2,1)} custom-call(bf16[8,2,48,256]{3,2,1,0:T(8,128)(2,1)S(1)} %all-to-all-done.r_ref), custom_call_target="tpu_custom_call" | custom-call | bytes 1000000 | tf_op jit(solution)/shard_map/pallas_call | solution.py:513
  38.3 3.6 %all-to-all-start.1 = ((bf16[8,2,48,256]{3,2,1,0:T(8,128)(2,1)}), bf16[8,2,48,256]{3,2,1,0:T(8,128)(2,1)S(1)}, u32[]{:S(2)}, u32[]{:S(2)}) async-start(bf16[8,2,48,256]{3,2,1,0:T(8,128)(2,1)} %shard_map.130), calls=%async_computation.1 | async-start | bytes 786432 | tf_op jit(solution)/shard_map/all_to_all | solution.py:594
  42.0 0.0 collective-permute-start.3
  42.0 11.9 %all-to-all-done.1 = bf16[8,2,48,256]{3,2,1,0:T(8,128)(2,1)S(1)} async-done(((bf16[8,2,48,256]{3,2,1,0:T(8,128)(2,1)}), bf16[8,2,48,256]{3,2,1,0:T(8,128)(2,1)S(1)}, u32[]{:S(2)}, u32[]{:S(2)}) %all-to-all-start.1) | async-done | bytes 393248 | tf_op jit(solution)/shard_map/all_to_all | solution.py:594
  53.8 0.0 collective-permute-start.4
  53.8 0.0 collective-permute-done.3.got_in
  53.8 0.0 copy-done.1
  53.8 0.0 copy-done
  53.9 1.6 %shard_map.132 = bf16[128,2048]{1,0:T(8,128)(2,1)} custom-call(bf16[512,512]{1,0:T(8,128)(2,1)S(1)} %copy-done.1, f32[16,2,4,16,128]{4,3,2,1,0:T(8,128)S(1)} %copy-done, bf16[16,2,4,16,128]{4,3,2,1,0:T(8,128)(2,1)S(1)} %collective-permute-done.3.got_in), custom_call_target="tpu_custom_call" | custom-call | flops 500000000 | bytes 4000000 | tf_op jit(solution)/shard_map/pallas_call | solution.py:513
  55.5 1.4 %shard_map.133 = (f32[112,512]{1,0:T(8,128)}, f32[112,512]{1,0:T(8,128)}) custom-call(bf16[16,48,256]{2,1,0:T(8,128)(2,1)S(1)} %bitcast.7), custom_call_target="tpu_custom_call" | custom-call | bytes 1000000 | tf_op jit(solution)/shard_map/pallas_call | solution.py:513
  56.9 0.0 collective-permute-done.4.got_ref
  56.9 1.4 %shard_map.134 = f32[28,4,512]{2,1,0:T(4,128)} custom-call(bf16[16,48,256]{2,1,0:T(8,128)(2,1)S(1)} %bitcast.8, bf16[16,48,256]{2,1,0:T(8,128)(2,1)S(1)} %collective-permute-done.4.got_ref), custom_call_target="tpu_custom_call" | custom-call | bytes 1000000 | tf_op jit(solution)/shard_map/pallas_call | solution.py:513
Async XLA Ops:
  0.6 3.4 %collective-permute-start.1 = (bf16[128,2048]{1,0:T(8,128)(2,1)}, bf16[128,2048]{1,0:T(8,128)(2,1)}, u32[]{:S(2)}, u32[]{:S(2)}) collective-permute-start(bf16[128,2048]{1,0:T(8,128)(2,1)} %x_own_in.1), channel_id=1, source_target_pairs={{0,1},{1,0},{2,3},{3,2},{4,5},{5,4},{6,7},{7,6},{8,9},{9,8},{10,11... | collective-permute-start | bytes 1572872 | tf_op jit(solution)/shard_map/ppermute | solution.py:538
  1.2 2.8 %collective-permute-start.2 = (bf16[128,2048]{1,0:T(8,128)(2,1)}, bf16[128,2048]{1,0:T(8,128)(2,1)}, u32[]{:S(2)}, u32[]{:S(2)}) collective-permute-start(bf16[128,2048]{1,0:T(8,128)(2,1)} %c_own_in.1), channel_id=1, source_target_pairs={{0,1},{1,0},{2,3},{3,2},{4,5},{5,4},{6,7},{7,6},{8,9},{9,8},{10,11... | collective-permute-start | bytes 1572872 | tf_op jit(solution)/shard_map/ppermute | solution.py:539
  1.3 2.7 %collective-permute-start = (bf16[28,4,512]{2,1,0:T(4,128)(2,1)}, bf16[28,4,512]{2,1,0:T(4,128)(2,1)}, u32[]{:S(2)}, u32[]{:S(2)}) collective-permute-start(bf16[28,4,512]{2,1,0:T(4,128)(2,1)} %bitcast.13), channel_id=1, source_target_pairs={{0,1},{1,0},{2,3},{3,2},{4,5},{5,4},{6,7},{7,6},{8,9},{9,8},{10,11... | collective-permute-start | bytes 344072 | tf_op jit(solution)/shard_map/ppermute | solution.py:541
  18.4 19.1 %all-to-all-start = ((bf16[8,2,48,256]{3,2,1,0:T(8,128)(2,1)}), bf16[8,2,48,256]{3,2,1,0:T(8,128)(2,1)S(1)}, u32[]{:S(2)}, u32[]{:S(2)}) async-start(bf16[8,2,48,256]{3,2,1,0:T(8,128)(2,1)} %bitcast.9), calls=%async_computation | async-start | bytes 786432 | tf_op jit(solution)/shard_map/all_to_all | solution.py:571
  25.5 28.3 %copy-start.1 = (bf16[512,512]{1,0:T(8,128)(2,1)S(1)}, bf16[512,512]{1,0:T(8,128)(2,1)}, u32[]{:S(2)}) copy-start(bf16[512,512]{1,0:T(8,128)(2,1)} %constant.11.clone.qt_in) | copy-start | bytes 1572868
  32.3 21.6 %copy-start = (f32[16,2,4,16,128]{4,3,2,1,0:T(8,128)S(1)}, f32[16,2,4,16,128]{4,3,2,1,0:T(8,128)}, u32[]{:S(2)}) copy-start(f32[16,2,4,16,128]{4,3,2,1,0:T(8,128)} %get-tuple-element.19.own_in) | copy-start | bytes 3145732
  38.3 15.5 %all-to-all-start.1 = ((bf16[8,2,48,256]{3,2,1,0:T(8,128)(2,1)}), bf16[8,2,48,256]{3,2,1,0:T(8,128)(2,1)S(1)}, u32[]{:S(2)}, u32[]{:S(2)}) async-start(bf16[8,2,48,256]{3,2,1,0:T(8,128)(2,1)} %shard_map.130), calls=%async_computation.1 | async-start | bytes 786432 | tf_op jit(solution)/shard_map/all_to_all | solution.py:594
  42.0 11.9 %collective-permute-start.3 = (bf16[16,2,4,16,128]{4,3,2,1,0:T(8,128)(2,1)}, bf16[16,2,4,16,128]{4,3,2,1,0:T(8,128)(2,1)S(1)}, u32[]{:S(2)}, u32[]{:S(2)}) collective-permute-start(bf16[16,2,4,16,128]{4,3,2,1,0:T(8,128)(2,1)} %get-tuple-element.20), channel_id=1, source_target_pairs={{0,1},{1,0},{2,3},{3,2},{4,5},{5,4},{6,7},{7,6},{8,9},{9,8},{10,11... | collective-permute-start | bytes 1572872 | tf_op jit(solution)/shard_map/ppermute | solution.py:595
  53.8 3.0 %collective-permute-start.4 = (bf16[16,48,256]{2,1,0:T(8,128)(2,1)S(1)}, bf16[16,48,256]{2,1,0:T(8,128)(2,1)S(1)}, u32[]{:S(2)}, u32[]{:S(2)}) collective-permute-start(bf16[16,48,256]{2,1,0:T(8,128)(2,1)S(1)} %bitcast.6), channel_id=1, source_target_pairs={{0,1},{1,0},{2,3},{3,2},{4,5},{5,4},{6,7},{7,6},{8,9},{9,8},{10,11... | collective-permute-start | bytes 1179656 | tf_op jit(solution)/shard_map/ppermute | solution.py:607

commit v2 on v1

--- a/solution.py
+++ b/solution.py
@@ -162,11 +162,13 @@
             two = side_by_side(result[..., j * LANES : (j + 2) * LANES])
             target[:, :, :, first // 2 + j // 2] = two.astype(jnp.bfloat16)
 
-    for copy in copies[:5]:
-        copy.wait()
-    to_spectra(x_own, sx, core * per)
-    to_spectra(c_own, sc, core * per)
     for n, (source, target) in enumerate(((wg_ref, rg), (wu_ref, ru))):
+        copies[n].wait()
+        if n:
+            for copy in copies[2:5]:
+                copy.wait()
+            to_spectra(x_own, sx, core * per)
+            to_spectra(c_own, sc, core * per)
         for tile in range(block // LANES):
             for o in range(fb):
                 flat[n, tile, o * db : (o + 1) * db] = source[o, :, tile * LANES : (tile + 1) * LANES].astype(jnp.float32)
@@ -476,8 +478,11 @@
     return jnp.where((lane == 0) & (part == 0), scale, 2.0 * scale)
 
 
-def layout_kernel(scale, fb, s_ref, gate_ref, up_ref, flat):
+def layout_kernel(scale, fb, s_ref, gate_out, up_out, gate_ref, up_ref, flat, out_sem):
     half = s_ref.shape[0] * PAIR
+    stores = [
+        pltpu.make_async_copy(src, dst, out_sem.at[w]) for w, (src, dst) in enumerate(((gate_ref, gate_out), (up_ref, up_out)))
+    ]
     for w, target in enumerate((gate_ref, up_ref)):
         for part in range(half // LANES):
             tiles = entries(s_ref, slice(w * ROWS, (w + 1) * ROWS), part)
@@ -486,6 +491,9 @@
                 for i in range(8):
                     flat[w, ri, pl.ds(i, fb, stride=8), :] = tiles[8 * ri + i][:fb] * factor(scale, part)
                 target[:, at : at + LANES] = flat[w, ri]
+        stores[w].start()
+    for copy in stores:
+        copy.wait()
 
 
 def down_layout_kernel(scale, fb, own_ref, got_ref, down_ref):
@@ -610,8 +618,10 @@
         functools.partial(layout_kernel, scale, fb),
         (shape((fb * db, block), f32),) * 2,
         (total,),
-        [pltpu.VMEM((2, 2, fb * db, LANES), f32)],
+        [pltpu.VMEM((fb * db, block), f32)] * 2
+        + [pltpu.VMEM((2, 2, fb * db, LANES), f32), pltpu.SemaphoreType.DMA((2,))],
         moved=10**6,
+        out_specs=(HBM,) * 2,
     )
     down_grad = call(
         functools.partial(down_layout_kernel, scale, fb),

time: 58.6 us -> 58.1 us (level)
  no operation moved by 1% of the time
where the time goes in v2:
time: 58.1 us; the launch traced here: 57.8 us
  Pallas kernels  25.8 us (44%)
  waiting for transfers between devices  19.4 us (33%)
  starting transfers between devices  11.9 us (20%)
  between operations  0.71 us (1%)
    pallas_call x6, Pallas kernels, call(): pl.pallas_call(kernel, out_shape=out_shape, in_specs=in_specs or [VMEM] *...  25.8 us
    all_to_all x1, waiting for transfers between devices, shards(): total = lax.all_to_all(total, 'dp', 0, 0, tiled=True)  11.9 us
    all_to_all x1, starting transfers between devices, shards(): lax.all_to_all(d_all.reshape(n_dp, share, 3 * ROWS, 2 * LANES), 'dp', 0,...  7.17 us
    all_to_all x1, waiting for transfers between devices, shards(): lax.all_to_all(d_all.reshape(n_dp, share, 3 * ROWS, 2 * LANES), 'dp', 0,...  5.23 us
    all_to_all x1, starting transfers between devices, shards(): total = lax.all_to_all(total, 'dp', 0, 0, tiled=True)  3.64 us
    ppermute x1, waiting for transfers between devices, shards(): down_got = lax.ppermute(down_own, 'mp', swap)  2.28 us
  transfers between devices with their start and end apart: 7, of which 3 were waited for; matrix products, arithmetic and copies ran while one was open for 0% of the time, Pallas kernels for 17%

profile of v2, /device:TPU:0, one launch (start us, length us, event | category | flops | bytes accessed | tf_op | source)
XLA Modules:
  0.0 57.8 jit_solution(8401102386101171614)
XLA Ops:
  0.6 0.6 collective-permute-start.1
  1.2 0.1 collective-permute-start.2
  1.3 0.4 collective-permute-start
  1.7 2.3 %collective-permute-done.wd_other_in = bf16[28,4,512]{2,1,0:T(4,128)(2,1)} collective-permute-done((bf16[28,4,512]{2,1,0:T(4,128)(2,1)}, bf16[28,4,512]{2,1,0:T(4,128)(2,1)}, u32[]{:S(2)}, u32[]{:S(2)}) %collective-permute-start) | collective-permute-done | bytes 114720 | tf_op jit(solution)/shard_map/ppermute | solution.py:549
  4.0 0.0 collective-permute-done.1.x_other_in
  4.0 0.0 collective-permute-done.2.c_other_in
  4.0 13.9 %shard_map.129 = (bf16[16,48,256]{2,1,0:T(8,128)(2,1)}, bf16[16,2,2,8,16,128]{5,4,3,2,1,0:T(8,128)(2,1)}, bf16[16,2,2,8,16,128]{5,4,3,2,1,0:T(8,128)(2,1)}) custom-call(bf16[14,8,512]{2,1,0:T(8,128)(2,1)} %wg_in.3, bf16[14,8,512]{2,1,0:T(8,128)(2,1)} %wu_in.3, bf16[512,512]{1,0:T(8,128)(2,1)} %constant.10.clone.pt_in, bf16[128,2048]{1,0:T(8,128)(2,1)} %x_own_in.1, ...), custom_call_target="tpu_custom_call" | custom-call | flops 10000000000 | bytes 10000000 | tf_op jit(solution)/shard_map/pallas_call | solution.py:521
  17.9 7.2 %all-to-all-start = ((bf16[8,2,48,256]{3,2,1,0:T(8,128)(2,1)}), bf16[8,2,48,256]{3,2,1,0:T(8,128)(2,1)S(1)}, u32[]{:S(2)}, u32[]{:S(2)}) async-start(bf16[8,2,48,256]{3,2,1,0:T(8,128)(2,1)} %bitcast.9), calls=%async_computation | async-start | bytes 786432 | tf_op jit(solution)/shard_map/all_to_all | solution.py:579
  25.0 0.0 copy-start.1
  25.0 6.7 %shard_map.131 = (f32[16,2,4,16,128]{4,3,2,1,0:T(8,128)}, bf16[16,2,4,16,128]{4,3,2,1,0:T(8,128)(2,1)}) custom-call(bf16[14,8,512]{2,1,0:T(8,128)(2,1)} %wg_in.3, bf16[14,8,512]{2,1,0:T(8,128)(2,1)} %wu_in.3, bf16[16,2,2,8,16,128]{5,4,3,2,1,0:T(8,128)(2,1)} %get-tuple-element.15.gg_in, bf16[16,2,2,8,16,128]{5,4,3,2,1,0:T(8,128)(2,1)} %get-tuple-element.16.ug_in), custom_call_target="tpu_custom_call" | custom-call | flops 2000000000 | bytes 10000000 | tf_op jit(solution)/shard_map/pallas_call | solution.py:521
  31.8 0.0 copy-start
  31.8 5.2 %all-to-all-done.r_ref = bf16[8,2,48,256]{3,2,1,0:T(8,128)(2,1)S(1)} async-done(((bf16[8,2,48,256]{3,2,1,0:T(8,128)(2,1)}), bf16[8,2,48,256]{3,2,1,0:T(8,128)(2,1)S(1)}, u32[]{:S(2)}, u32[]{:S(2)}) %all-to-all-start) | async-done | bytes 393248 | tf_op jit(solution)/shard_map/all_to_all | solution.py:579
  37.0 0.8 %shard_map.130 = bf16[8,2,48,256]{3,2,1,0:T(8,128)(2,1)} custom-call(bf16[8,2,48,256]{3,2,1,0:T(8,128)(2,1)S(1)} %all-to-all-done.r_ref), custom_call_target="tpu_custom_call" | custom-call | bytes 1000000 | tf_op jit(solution)/shard_map/pallas_call | solution.py:521
  37.8 3.6 %all-to-all-start.1 = ((bf16[8,2,48,256]{3,2,1,0:T(8,128)(2,1)}), bf16[8,2,48,256]{3,2,1,0:T(8,128)(2,1)S(1)}, u32[]{:S(2)}, u32[]{:S(2)}) async-start(bf16[8,2,48,256]{3,2,1,0:T(8,128)(2,1)} %shard_map.130), calls=%async_computation.1 | async-start | bytes 786432 | tf_op jit(solution)/shard_map/all_to_all | solution.py:602
  41.5 0.0 collective-permute-start.3
  41.5 11.9 %all-to-all-done.1 = bf16[8,2,48,256]{3,2,1,0:T(8,128)(2,1)S(1)} async-done(((bf16[8,2,48,256]{3,2,1,0:T(8,128)(2,1)}), bf16[8,2,48,256]{3,2,1,0:T(8,128)(2,1)S(1)}, u32[]{:S(2)}, u32[]{:S(2)}) %all-to-all-start.1) | async-done | bytes 393248 | tf_op jit(solution)/shard_map/all_to_all | solution.py:602
  53.3 0.0 collective-permute-start.4
  53.3 0.0 collective-permute-done.3.got_in
  53.3 0.0 copy-done.1
  53.3 0.0 copy-done
  53.4 1.6 %shard_map.132 = bf16[128,2048]{1,0:T(8,128)(2,1)} custom-call(bf16[512,512]{1,0:T(8,128)(2,1)S(1)} %copy-done.1, f32[16,2,4,16,128]{4,3,2,1,0:T(8,128)S(1)} %copy-done, bf16[16,2,4,16,128]{4,3,2,1,0:T(8,128)(2,1)S(1)} %collective-permute-done.3.got_in), custom_call_target="tpu_custom_call" | custom-call | flops 500000000 | bytes 4000000 | tf_op jit(solution)/shard_map/pallas_call | solution.py:521
  55.0 1.4 %shard_map.133 = (f32[112,512]{1,0:T(8,128)}, f32[112,512]{1,0:T(8,128)}) custom-call(bf16[16,48,256]{2,1,0:T(8,128)(2,1)S(1)} %bitcast.7), custom_call_target="tpu_custom_call" | custom-call | bytes 1000000 | tf_op jit(solution)/shard_map/pallas_call | solution.py:521
  56.4 0.0 collective-permute-done.4.got_ref
  56.4 1.4 %shard_map.134 = f32[28,4,512]{2,1,0:T(4,128)} custom-call(bf16[16,48,256]{2,1,0:T(8,128)(2,1)S(1)} %bitcast.8, bf16[16,48,256]{2,1,0:T(8,128)(2,1)S(1)} %collective-permute-done.4.got_ref), custom_call_target="tpu_custom_call" | custom-call | bytes 1000000 | tf_op jit(solution)/shard_map/pallas_call | solution.py:521
Async XLA Ops:
  0.6 3.4 %collective-permute-start.1 = (bf16[128,2048]{1,0:T(8,128)(2,1)}, bf16[128,2048]{1,0:T(8,128)(2,1)}, u32[]{:S(2)}, u32[]{:S(2)}) collective-permute-start(bf16[128,2048]{1,0:T(8,128)(2,1)} %x_own_in.1), channel_id=1, source_target_pairs={{0,1},{1,0},{2,3},{3,2},{4,5},{5,4},{6,7},{7,6},{8,9},{9,8},{10,11... | collective-permute-start | bytes 1572872 | tf_op jit(solution)/shard_map/ppermute | solution.py:546
  1.2 2.8 %collective-permute-start.2 = (bf16[128,2048]{1,0:T(8,128)(2,1)}, bf16[128,2048]{1,0:T(8,128)(2,1)}, u32[]{:S(2)}, u32[]{:S(2)}) collective-permute-start(bf16[128,2048]{1,0:T(8,128)(2,1)} %c_own_in.1), channel_id=1, source_target_pairs={{0,1},{1,0},{2,3},{3,2},{4,5},{5,4},{6,7},{7,6},{8,9},{9,8},{10,11... | collective-permute-start | bytes 1572872 | tf_op jit(solution)/shard_map/ppermute | solution.py:547
  1.3 2.7 %collective-permute-start = (bf16[28,4,512]{2,1,0:T(4,128)(2,1)}, bf16[28,4,512]{2,1,0:T(4,128)(2,1)}, u32[]{:S(2)}, u32[]{:S(2)}) collective-permute-start(bf16[28,4,512]{2,1,0:T(4,128)(2,1)} %bitcast.13), channel_id=1, source_target_pairs={{0,1},{1,0},{2,3},{3,2},{4,5},{5,4},{6,7},{7,6},{8,9},{9,8},{10,11... | collective-permute-start | bytes 344072 | tf_op jit(solution)/shard_map/ppermute | solution.py:549
  17.9 19.2 %all-to-all-start = ((bf16[8,2,48,256]{3,2,1,0:T(8,128)(2,1)}), bf16[8,2,48,256]{3,2,1,0:T(8,128)(2,1)S(1)}, u32[]{:S(2)}, u32[]{:S(2)}) async-start(bf16[8,2,48,256]{3,2,1,0:T(8,128)(2,1)} %bitcast.9), calls=%async_computation | async-start | bytes 786432 | tf_op jit(solution)/shard_map/all_to_all | solution.py:579
  25.0 28.3 %copy-start.1 = (bf16[512,512]{1,0:T(8,128)(2,1)S(1)}, bf16[512,512]{1,0:T(8,128)(2,1)}, u32[]{:S(2)}) copy-start(bf16[512,512]{1,0:T(8,128)(2,1)} %constant.11.clone.qt_in) | copy-start | bytes 1572868
  31.8 21.6 %copy-start = (f32[16,2,4,16,128]{4,3,2,1,0:T(8,128)S(1)}, f32[16,2,4,16,128]{4,3,2,1,0:T(8,128)}, u32[]{:S(2)}) copy-start(f32[16,2,4,16,128]{4,3,2,1,0:T(8,128)} %get-tuple-element.19.own_in) | copy-start | bytes 3145732
  37.8 15.5 %all-to-all-start.1 = ((bf16[8,2,48,256]{3,2,1,0:T(8,128)(2,1)}), bf16[8,2,48,256]{3,2,1,0:T(8,128)(2,1)S(1)}, u32[]{:S(2)}, u32[]{:S(2)}) async-start(bf16[8,2,48,256]{3,2,1,0:T(8,128)(2,1)} %shard_map.130), calls=%async_computation.1 | async-start | bytes 786432 | tf_op jit(solution)/shard_map/all_to_all | solution.py:602
  41.5 11.9 %collective-permute-start.3 = (bf16[16,2,4,16,128]{4,3,2,1,0:T(8,128)(2,1)}, bf16[16,2,4,16,128]{4,3,2,1,0:T(8,128)(2,1)S(1)}, u32[]{:S(2)}, u32[]{:S(2)}) collective-permute-start(bf16[16,2,4,16,128]{4,3,2,1,0:T(8,128)(2,1)} %get-tuple-element.20), channel_id=1, source_target_pairs={{0,1},{1,0},{2,3},{3,2},{4,5},{5,4},{6,7},{7,6},{8,9},{9,8},{10,11... | collective-permute-start | bytes 1572872 | tf_op jit(solution)/shard_map/ppermute | solution.py:603
  53.3 3.1 %collective-permute-start.4 = (bf16[16,48,256]{2,1,0:T(8,128)(2,1)S(1)}, bf16[16,48,256]{2,1,0:T(8,128)(2,1)S(1)}, u32[]{:S(2)}, u32[]{:S(2)}) collective-permute-start(bf16[16,48,256]{2,1,0:T(8,128)(2,1)S(1)} %bitcast.6), channel_id=1, source_target_pairs={{0,1},{1,0},{2,3},{3,2},{4,5},{5,4},{6,7},{7,6},{8,9},{9,8},{10,11... | collective-permute-start | bytes 1179656 | tf_op jit(solution)/shard_map/ppermute | solution.py:615

commit v3 on v2

--- a/solution.py
+++ b/solution.py
@@ -190,7 +190,7 @@
     for side in range(2):
         for tile in range(block // LANES):
             rows = wd_ref[side, :, :, tile * LANES : (tile + 1) * LANES].astype(jnp.float32)
-            flat_down[side, tile] = rows.reshape(2 * fb * per, LANES)
+            flat_down[side, tile, : 2 * fb * per] = rows.reshape(2 * fb * per, LANES)
 
     def read_down(o, at):
         return flat_down[o // per, at // LANES, pl.ds(core * fb * per + o % per, fb, stride=per), :]
@@ -490,7 +490,7 @@
                 at = ri * half + part * LANES
                 for i in range(8):
                     flat[w, ri, pl.ds(i, fb, stride=8), :] = tiles[8 * ri + i][:fb] * factor(scale, part)
-                target[:, at : at + LANES] = flat[w, ri]
+                target[:, at : at + LANES] = flat[w, ri, : 8 * fb]
         stores[w].start()
     for copy in stores:
         copy.wait()
@@ -561,10 +561,10 @@
         + [pltpu.VMEM((pairs, 2, 2, db // 2, PAIR, LANES), bf16)] * 2
         + [pltpu.VMEM((fb, pairs, 2, PAIR, LANES), bf16)] * 3
         + [pltpu.VMEM(spec.shape, bf16)] * 3
-        + [pltpu.VMEM((groups * 2 * ROWS, LANES), f32)] * 3
+        + [pltpu.VMEM((groups * 2 * ROWS + F, LANES), f32)] * 3
         + [pltpu.VMEM((2, 3, half, 2 * LANES), bf16)] * 2
-        + [pltpu.VMEM((2, 3, F, 2 * LANES), f32), pltpu.VMEM((2, block // LANES, fb * db, LANES), f32)]
-        + [pltpu.VMEM((2, block // LANES, 2 * fb * per, LANES), f32), pltpu.VMEM((pairs, 3 * ROWS, 2 * LANES), bf16)]
+        + [pltpu.VMEM((2, 3, F, 2 * LANES), f32), pltpu.VMEM((2, block // LANES, ROWS * db, LANES), f32)]
+        + [pltpu.VMEM((2, block // LANES, 2 * ROWS * per, LANES), f32), pltpu.VMEM((pairs, 3 * ROWS, 2 * LANES), bf16)]
         + [pltpu.SemaphoreType.DMA((n,)) for n in (len(inputs), 2, pairs // 8)],
         limit=ALL_VMEM,
         flops=10**10,
@@ -586,7 +586,7 @@
         (gate_spectra, up_spectra, gg, ug),
         [pltpu.VMEM(gate_spectra.shape, bf16)] * 2
         + [pltpu.VMEM(spec.shape, bf16)] * 2
-        + [pltpu.VMEM((2, groups * 2 * db, LANES), f32)] * 2
+        + [pltpu.VMEM((2, groups * 2 * db + F, LANES), f32)] * 2
         + [pltpu.VMEM((2, 2, db, PAIR, LANES), f32)]
         + [pltpu.VMEM((pairs, 2, per, PAIR, LANES), t) for t in (f32, bf16)]
         + [pltpu.SemaphoreType.DMA(n) for n in ((2,), (2, pairs), (2, pairs // 2))],
@@ -619,7 +619,7 @@
         (shape((fb * db, block), f32),) * 2,
         (total,),
         [pltpu.VMEM((fb * db, block), f32)] * 2
-        + [pltpu.VMEM((2, 2, fb * db, LANES), f32), pltpu.SemaphoreType.DMA((2,))],
+        + [pltpu.VMEM((2, 2, ROWS * db, LANES), f32), pltpu.SemaphoreType.DMA((2,))],
         moved=10**6,
         out_specs=(HBM,) * 2,
     )

time: 58.1 us -> 58.1 us (level)
  no operation moved by 1% of the time
where the time goes in v3:
time: 58.1 us; the launch traced here: 57.8 us
  Pallas kernels  25.9 us (45%)
  waiting for transfers between devices  19.3 us (33%)
  starting transfers between devices  11.9 us (20%)
  between operations  0.71 us (1%)
    pallas_call x6, Pallas kernels, call(): pl.pallas_call(kernel, out_shape=out_shape, in_specs=in_specs or [VMEM] *...  25.9 us
    all_to_all x1, waiting for transfers between devices, shards(): total = lax.all_to_all(total, 'dp', 0, 0, tiled=True)  11.9 us
    all_to_all x1, starting transfers between devices, shards(): lax.all_to_all(d_all.reshape(n_dp, share, 3 * ROWS, 2 * LANES), 'dp', 0,...  7.17 us
    all_to_all x1, waiting for transfers between devices, shards(): lax.all_to_all(d_all.reshape(n_dp, share, 3 * ROWS, 2 * LANES), 'dp', 0,...  5.16 us
    all_to_all x1, starting transfers between devices, shards(): total = lax.all_to_all(total, 'dp', 0, 0, tiled=True)  3.64 us
    ppermute x1, waiting for transfers between devices, shards(): down_got = lax.ppermute(down_own, 'mp', swap)  2.28 us
  transfers between devices with their start and end apart: 7, of which 3 were waited for; matrix products, arithmetic and copies ran while one was open for 0% of the time, Pallas kernels for 17%

profile of v3, /device:TPU:0, one launch (start us, length us, event | category | flops | bytes accessed | tf_op | source)
XLA Modules:
  0.0 57.8 jit_solution(16708873960586957951)
XLA Ops:
  0.6 0.6 collective-permute-start.1
  1.2 0.1 collective-permute-start.2
  1.3 0.4 collective-permute-start
  1.7 2.3 %collective-permute-done.wd_other_in = bf16[28,4,512]{2,1,0:T(4,128)(2,1)} collective-permute-done((bf16[28,4,512]{2,1,0:T(4,128)(2,1)}, bf16[28,4,512]{2,1,0:T(4,128)(2,1)}, u32[]{:S(2)}, u32[]{:S(2)}) %collective-permute-start) | collective-permute-done | bytes 114720 | tf_op jit(solution)/shard_map/ppermute | solution.py:549
  4.0 0.0 collective-permute-done.1.x_other_in
  4.0 0.0 collective-permute-done.2.c_other_in
  4.0 13.9 %shard_map.129 = (bf16[16,48,256]{2,1,0:T(8,128)(2,1)}, bf16[16,2,2,8,16,128]{5,4,3,2,1,0:T(8,128)(2,1)}, bf16[16,2,2,8,16,128]{5,4,3,2,1,0:T(8,128)(2,1)}) custom-call(bf16[14,8,512]{2,1,0:T(8,128)(2,1)} %wg_in.3, bf16[14,8,512]{2,1,0:T(8,128)(2,1)} %wu_in.3, bf16[512,512]{1,0:T(8,128)(2,1)} %constant.10.clone.pt_in, bf16[128,2048]{1,0:T(8,128)(2,1)} %x_own_in.1, ...), custom_call_target="tpu_custom_call" | custom-call | flops 10000000000 | bytes 10000000 | tf_op jit(solution)/shard_map/pallas_call | solution.py:521
  17.9 7.2 %all-to-all-start = ((bf16[8,2,48,256]{3,2,1,0:T(8,128)(2,1)}), bf16[8,2,48,256]{3,2,1,0:T(8,128)(2,1)S(1)}, u32[]{:S(2)}, u32[]{:S(2)}) async-start(bf16[8,2,48,256]{3,2,1,0:T(8,128)(2,1)} %bitcast.9), calls=%async_computation | async-start | bytes 786432 | tf_op jit(solution)/shard_map/all_to_all | solution.py:579
  25.1 0.0 copy-start.1
  25.1 6.8 %shard_map.131 = (f32[16,2,4,16,128]{4,3,2,1,0:T(8,128)}, bf16[16,2,4,16,128]{4,3,2,1,0:T(8,128)(2,1)}) custom-call(bf16[14,8,512]{2,1,0:T(8,128)(2,1)} %wg_in.3, bf16[14,8,512]{2,1,0:T(8,128)(2,1)} %wu_in.3, bf16[16,2,2,8,16,128]{5,4,3,2,1,0:T(8,128)(2,1)} %get-tuple-element.15.gg_in, bf16[16,2,2,8,16,128]{5,4,3,2,1,0:T(8,128)(2,1)} %get-tuple-element.16.ug_in), custom_call_target="tpu_custom_call" | custom-call | flops 2000000000 | bytes 10000000 | tf_op jit(solution)/shard_map/pallas_call | solution.py:521
  31.9 0.0 copy-start
  31.9 5.2 %all-to-all-done.r_ref = bf16[8,2,48,256]{3,2,1,0:T(8,128)(2,1)S(1)} async-done(((bf16[8,2,48,256]{3,2,1,0:T(8,128)(2,1)}), bf16[8,2,48,256]{3,2,1,0:T(8,128)(2,1)S(1)}, u32[]{:S(2)}, u32[]{:S(2)}) %all-to-all-start) | async-done | bytes 393248 | tf_op jit(solution)/shard_map/all_to_all | solution.py:579
  37.0 0.8 %shard_map.130 = bf16[8,2,48,256]{3,2,1,0:T(8,128)(2,1)} custom-call(bf16[8,2,48,256]{3,2,1,0:T(8,128)(2,1)S(1)} %all-to-all-done.r_ref), custom_call_target="tpu_custom_call" | custom-call | bytes 1000000 | tf_op jit(solution)/shard_map/pallas_call | solution.py:521
  37.8 3.6 %all-to-all-start.1 = ((bf16[8,2,48,256]{3,2,1,0:T(8,128)(2,1)}), bf16[8,2,48,256]{3,2,1,0:T(8,128)(2,1)S(1)}, u32[]{:S(2)}, u32[]{:S(2)}) async-start(bf16[8,2,48,256]{3,2,1,0:T(8,128)(2,1)} %shard_map.130), calls=%async_computation.1 | async-start | bytes 786432 | tf_op jit(solution)/shard_map/all_to_all | solution.py:602
  41.5 0.0 collective-permute-start.3
  41.5 11.9 %all-to-all-done.1 = bf16[8,2,48,256]{3,2,1,0:T(8,128)(2,1)S(1)} async-done(((bf16[8,2,48,256]{3,2,1,0:T(8,128)(2,1)}), bf16[8,2,48,256]{3,2,1,0:T(8,128)(2,1)S(1)}, u32[]{:S(2)}, u32[]{:S(2)}) %all-to-all-start.1) | async-done | bytes 393248 | tf_op jit(solution)/shard_map/all_to_all | solution.py:602
  53.3 0.0 collective-permute-start.4
  53.3 0.0 collective-permute-done.3.got_in
  53.3 0.0 copy-done.1
  53.4 0.0 copy-done
  53.4 1.6 %shard_map.132 = bf16[128,2048]{1,0:T(8,128)(2,1)} custom-call(bf16[512,512]{1,0:T(8,128)(2,1)S(1)} %copy-done.1, f32[16,2,4,16,128]{4,3,2,1,0:T(8,128)S(1)} %copy-done, bf16[16,2,4,16,128]{4,3,2,1,0:T(8,128)(2,1)S(1)} %collective-permute-done.3.got_in), custom_call_target="tpu_custom_call" | custom-call | flops 500000000 | bytes 4000000 | tf_op jit(solution)/shard_map/pallas_call | solution.py:521
  55.0 1.4 %shard_map.133 = (f32[112,512]{1,0:T(8,128)}, f32[112,512]{1,0:T(8,128)}) custom-call(bf16[16,48,256]{2,1,0:T(8,128)(2,1)S(1)} %bitcast.7), custom_call_target="tpu_custom_call" | custom-call | bytes 1000000 | tf_op jit(solution)/shard_map/pallas_call | solution.py:521
  56.4 0.0 collective-permute-done.4.got_ref
  56.4 1.4 %shard_map.134 = f32[28,4,512]{2,1,0:T(4,128)} custom-call(bf16[16,48,256]{2,1,0:T(8,128)(2,1)S(1)} %bitcast.8, bf16[16,48,256]{2,1,0:T(8,128)(2,1)S(1)} %collective-permute-done.4.got_ref), custom_call_target="tpu_custom_call" | custom-call | bytes 1000000 | tf_op jit(solution)/shard_map/pallas_call | solution.py:521
Async XLA Ops:
  0.6 3.4 %collective-permute-start.1 = (bf16[128,2048]{1,0:T(8,128)(2,1)}, bf16[128,2048]{1,0:T(8,128)(2,1)}, u32[]{:S(2)}, u32[]{:S(2)}) collective-permute-start(bf16[128,2048]{1,0:T(8,128)(2,1)} %x_own_in.1), channel_id=1, source_target_pairs={{0,1},{1,0},{2,3},{3,2},{4,5},{5,4},{6,7},{7,6},{8,9},{9,8},{10,11... | collective-permute-start | bytes 1572872 | tf_op jit(solution)/shard_map/ppermute | solution.py:546
  1.2 2.8 %collective-permute-start.2 = (bf16[128,2048]{1,0:T(8,128)(2,1)}, bf16[128,2048]{1,0:T(8,128)(2,1)}, u32[]{:S(2)}, u32[]{:S(2)}) collective-permute-start(bf16[128,2048]{1,0:T(8,128)(2,1)} %c_own_in.1), channel_id=1, source_target_pairs={{0,1},{1,0},{2,3},{3,2},{4,5},{5,4},{6,7},{7,6},{8,9},{9,8},{10,11... | collective-permute-start | bytes 1572872 | tf_op jit(solution)/shard_map/ppermute | solution.py:547
  1.3 2.7 %collective-permute-start = (bf16[28,4,512]{2,1,0:T(4,128)(2,1)}, bf16[28,4,512]{2,1,0:T(4,128)(2,1)}, u32[]{:S(2)}, u32[]{:S(2)}) collective-permute-start(bf16[28,4,512]{2,1,0:T(4,128)(2,1)} %bitcast.13), channel_id=1, source_target_pairs={{0,1},{1,0},{2,3},{3,2},{4,5},{5,4},{6,7},{7,6},{8,9},{9,8},{10,11... | collective-permute-start | bytes 344072 | tf_op jit(solution)/shard_map/ppermute | solution.py:549
  17.9 19.1 %all-to-all-start = ((bf16[8,2,48,256]{3,2,1,0:T(8,128)(2,1)}), bf16[8,2,48,256]{3,2,1,0:T(8,128)(2,1)S(1)}, u32[]{:S(2)}, u32[]{:S(2)}) async-start(bf16[8,2,48,256]{3,2,1,0:T(8,128)(2,1)} %bitcast.9), calls=%async_computation | async-start | bytes 786432 | tf_op jit(solution)/shard_map/all_to_all | solution.py:579
  25.1 28.3 %copy-start.1 = (bf16[512,512]{1,0:T(8,128)(2,1)S(1)}, bf16[512,512]{1,0:T(8,128)(2,1)}, u32[]{:S(2)}) copy-start(bf16[512,512]{1,0:T(8,128)(2,1)} %constant.11.clone.qt_in) | copy-start | bytes 1572868
  31.9 21.5 %copy-start = (f32[16,2,4,16,128]{4,3,2,1,0:T(8,128)S(1)}, f32[16,2,4,16,128]{4,3,2,1,0:T(8,128)}, u32[]{:S(2)}) copy-start(f32[16,2,4,16,128]{4,3,2,1,0:T(8,128)} %get-tuple-element.19.own_in) | copy-start | bytes 3145732
  37.8 15.5 %all-to-all-start.1 = ((bf16[8,2,48,256]{3,2,1,0:T(8,128)(2,1)}), bf16[8,2,48,256]{3,2,1,0:T(8,128)(2,1)S(1)}, u32[]{:S(2)}, u32[]{:S(2)}) async-start(bf16[8,2,48,256]{3,2,1,0:T(8,128)(2,1)} %shard_map.130), calls=%async_computation.1 | async-start | bytes 786432 | tf_op jit(solution)/shard_map/all_to_all | solution.py:602
  41.5 11.9 %collective-permute-start.3 = (bf16[16,2,4,16,128]{4,3,2,1,0:T(8,128)(2,1)}, bf16[16,2,4,16,128]{4,3,2,1,0:T(8,128)(2,1)S(1)}, u32[]{:S(2)}, u32[]{:S(2)}) collective-permute-start(bf16[16,2,4,16,128]{4,3,2,1,0:T(8,128)(2,1)} %get-tuple-element.20), channel_id=1, source_target_pairs={{0,1},{1,0},{2,3},{3,2},{4,5},{5,4},{6,7},{7,6},{8,9},{9,8},{10,11... | collective-permute-start | bytes 1572872 | tf_op jit(solution)/shard_map/ppermute | solution.py:603
  53.3 3.1 %collective-permute-start.4 = (bf16[16,48,256]{2,1,0:T(8,128)(2,1)S(1)}, bf16[16,48,256]{2,1,0:T(8,128)(2,1)S(1)}, u32[]{:S(2)}, u32[]{:S(2)}) collective-permute-start(bf16[16,48,256]{2,1,0:T(8,128)(2,1)S(1)} %bitcast.6), channel_id=1, source_target_pairs={{0,1},{1,0},{2,3},{3,2},{4,5},{5,4},{6,7},{7,6},{8,9},{9,8},{10,11... | collective-permute-start | bytes 1179656 | tf_op jit(solution)/shard_map/ppermute | solution.py:615
